TPU v7x, 32 devices: a whole 2x2x4 slice. The times are simulated.
32 devices in a mesh: parts: 2 (over y), dp: 4 (over z), tensor: 4 (over x, core).
Axes of the slice: x: 2, y: 2, z: 4, core: 2. Of those that a mesh axis runs over, the one named last changes fastest.
Arguments:
- prompt_kv: bfloat16 [2, 14336, 8, 128], P(None, ('parts', 'dp'), 'tensor'), parts along dimension 1, may hold values from -12 to 12
- gen_kv: bfloat16 [64, 2, 128, 8, 128], P(('parts', 'dp'), None, None, 'tensor'), parts along dimension 0, may hold values from -17 to 17
- queries: bfloat16 [2, 64, 64, 128], P(None, ('parts', 'dp'), 'tensor'), parts along dimension 1, may hold values from -24 to 24
- new_kv: bfloat16 [2, 2, 64, 8, 128], P(None, None, ('parts', 'dp'), 'tensor'), parts along dimension 2, may hold values from -48 to 48
- ancestors: int32 [64], P(('parts', 'dp')), parts along dimension 0, may hold values from 0 to 31, as said below
- prior_twist: float32 [64], P(('parts', 'dp')), parts along dimension 0, may hold values from -290 to 6
- twist_vec: float32 [64, 128], P('tensor'), may hold values from -1 to 1
Outputs:
- attended: bfloat16 [2, 64, 64, 128], P(None, ('parts', 'dp'), 'tensor'), parts along dimension 1
- log_weights: float32 [64], P(('parts', 'dp')), parts along dimension 0
There are 2 independent parts, one for each index of `parts`. A program takes and returns all parts, laid end to end along the dimension named above; an argument that names none is the same for every part. Nothing has to cross between parts.
Inputs may be any that keep to these rules, and one draw needn't show every extreme that they name: Duplicates are allowed. Among the 8 particles of one device (equal p // 8) at most 4 have ancestors held by one same device (equal ancestors // 8), and every device has exactly 4 from some device.
All inputs are finite; a program needn't handle non-finite values.
Results may differ from a plain program's by a relative error of at most 0.0017.
Values may be sent and summed in bfloat16 or wider, within the bound.
A program may use at most 128 MiB of HBM per device.

v0:
```python
import math

import jax
import jax.numpy as jnp
from jax import lax
from jax.sharding import PartitionSpec as P


def join_states(left_state, right_state):
    largest = jnp.maximum(left_state[0], right_state[0])
    left_scale = jnp.exp(left_state[0] - largest)
    right_scale = jnp.exp(right_state[0] - largest)
    return (
        largest,
        left_state[1] * left_scale + right_state[1] * right_scale,
        left_state[2] * left_scale[..., None] + right_state[2] * right_scale[..., None],
    )


def fold_blocks(moments, totals, weighted, along):
    largest = jnp.max(moments, axis=along)
    scale_each = jnp.exp(moments - jnp.expand_dims(largest, along))
    return (
        largest,
        jnp.sum(totals * scale_each, axis=along),
        jnp.sum(weighted * scale_each[..., None], axis=along),
    )


def block_state(scores, values, pattern):
    largest = jnp.max(scores, axis=-1)
    exponent = jnp.exp(scores - largest[..., None])
    weighted = jnp.einsum(
        pattern, exponent.astype(jnp.bfloat16), values, preferred_element_type=jnp.float32
    )
    return (largest, jnp.sum(exponent, axis=-1), weighted)


def prompt_states(query_rows, prompt_kv, kv_count, scaling):
    row_count, head_count, head_size = query_rows.shape
    group_size = head_count // kv_count
    per_block = math.gcd(row_count, 256)
    blocked = query_rows.reshape(row_count // per_block, per_block, kv_count, group_size, head_size)
    key_rows = prompt_kv[0]
    values = prompt_kv[1]

    def attend_block(query_block):
        scores = (
            jnp.einsum("pcgd,kcd->pcgk", query_block, key_rows, preferred_element_type=jnp.float32)
            * scaling
        )
        return block_state(scores, values, "pcgk,kcd->pcgd")

    largest, totals, weighted = lax.map(attend_block, blocked)
    return (
        largest.reshape(row_count, head_count),
        totals.reshape(row_count, head_count),
        weighted.reshape(row_count, head_count, head_size),
    )


def per_device(prompt_kv, gen_kv, queries, new_kv, ancestors, prior_twist, twist_vec):
    step_count, local_count, head_count, head_size = queries.shape
    kv_count = prompt_kv.shape[2]
    group_size = head_count // kv_count
    scaling = 1.0 / math.sqrt(head_size)
    devices = lax.axis_size("dp")
    capacity = max(2, (2 * local_count + devices - 1) // devices)
    slot_total = devices * capacity
    source = ancestors // local_count
    offset = ancestors % local_count
    places = jnp.arange(local_count)
    earlier = (source[:, None] == source[None, :]) & (places[None, :] < places[:, None])
    arrival_rank = jnp.sum(earlier.astype(jnp.int32), axis=1)
    slot_index = source * capacity + arrival_rank
    slot_match = jnp.arange(slot_total)[:, None] == slot_index[None, :]
    wanted = jnp.sum(jnp.where(slot_match, offset[None, :] + 1, 0), axis=1) - 1
    requests_in = lax.all_to_all(
        wanted.reshape(devices, capacity), "dp", split_axis=0, concat_axis=0, tiled=True
    )
    picked = jnp.clip(requests_in, 0, local_count - 1).reshape(-1)
    every_prior = lax.all_gather(prior_twist, "dp", axis=0, tiled=True)
    twist_before = jnp.take(every_prior, ancestors, axis=0)
    split_query = queries.reshape(step_count, local_count, kv_count, group_size, head_size)
    sent_rows = jnp.take(gen_kv, picked, axis=0).reshape((devices, capacity) + gen_kv.shape[1:])
    arrived = lax.all_to_all(sent_rows, "dp", split_axis=0, concat_axis=0, tiled=True)
    resampled = jnp.take(arrived.reshape((slot_total,) + gen_kv.shape[1:]), slot_index, axis=0)
    cache_scores = (
        jnp.einsum(
            "spcgd,pkcd->spcgk", split_query, resampled[:, 0], preferred_element_type=jnp.float32
        )
        * scaling
    )
    largest, totals, weighted = block_state(cache_scores, resampled[:, 1], "spcgk,pkcd->spcgd")
    cached = (
        largest.reshape(step_count, local_count, head_count),
        totals.reshape(step_count, local_count, head_count),
        weighted.reshape(step_count, local_count, head_count, head_size),
    )
    new_scores = (
        jnp.einsum(
            "spcgd,tpcd->spcgt", split_query, new_kv[:, 0], preferred_element_type=jnp.float32
        )
        * scaling
    )
    positions = jnp.arange(step_count)
    allowed = positions[None, :] <= positions[:, None]
    new_scores = jnp.where(allowed[:, None, None, None, :], new_scores, -jnp.inf)
    largest, totals, weighted = block_state(new_scores, new_kv[:, 1], "spcgt,tpcd->spcgd")
    fresh_state = (
        largest.reshape(step_count, local_count, head_count),
        totals.reshape(step_count, local_count, head_count),
        weighted.reshape(step_count, local_count, head_count, head_size),
    )
    everyone = lax.all_gather(queries, "dp", axis=1, tiled=True)
    largest, totals, weighted = prompt_states(
        everyone.reshape(step_count * devices * local_count, head_count, head_size),
        prompt_kv,
        kv_count,
        scaling,
    )
    arrived_states = (
        lax.all_to_all(
            largest.reshape(step_count, devices, local_count, head_count),
            "dp",
            split_axis=1,
            concat_axis=1,
            tiled=True,
        ),
        lax.all_to_all(
            totals.reshape(step_count, devices, local_count, head_count),
            "dp",
            split_axis=1,
            concat_axis=1,
            tiled=True,
        ),
        lax.all_to_all(
            weighted.reshape(step_count, devices, local_count, head_count, head_size),
            "dp",
            split_axis=1,
            concat_axis=1,
            tiled=True,
        ),
    )
    prompt_state = fold_blocks(arrived_states[0], arrived_states[1], arrived_states[2], 1)
    joined = join_states(join_states(prompt_state, cached), fresh_state)
    attended = (joined[2] / joined[1][..., None]).astype(jnp.bfloat16)
    last_step = lax.optimization_barrier(attended[-1]).astype(jnp.float32)
    local_twist = jnp.sum(last_step * twist_vec, axis=(1, 2))
    twist_value = lax.psum(local_twist, "tensor")
    raw_weight = twist_value - twist_before
    largest_weight = lax.pmax(jnp.max(raw_weight), "dp")
    weight_mass = lax.psum(jnp.sum(jnp.exp(raw_weight - largest_weight)), "dp")
    normalizer = largest_weight + jnp.log(weight_mass)
    return (attended, raw_weight - normalizer)


def solution(mesh):
    placed = (
        P(None, ("parts", "dp"), "tensor", None),
        P(("parts", "dp"), None, None, "tensor", None),
        P(None, ("parts", "dp"), "tensor", None),
        P(None, None, ("parts", "dp"), "tensor", None),
        P(("parts", "dp")),
        P(("parts", "dp")),
        P("tensor", None),
    )
    return jax.shard_map(
        per_device,
        mesh=mesh,
        in_specs=placed,
        out_specs=(P(None, ("parts", "dp"), "tensor", None), P(("parts", "dp"))),
        check_vma=False,
    )
```

profile of v0, /device:TPU:0, one launch (start us, length us, event | category | flops | bytes accessed | tf_op | source)
XLA Modules:
  0.0 157.3 jit_solution(7130623179860953342)
XLA Ops:
  0.6 0.8 compare_select_fusion.3
  1.7 0.7 sub.106
  2.4 6.3 %all-to-all-start.2 = ((s32[4,1,4]{2,1,0:T(1,128)}), s32[4,1,4]{2,1,0:T(1,128)S(1)}, u32[]{:S(2)}, u32[]{:S(2)}) async-start(s32[4,1,4]{2,1,0:T(1,128)} %bitcast.10), calls=%async_computation.2 | async-start | bytes 4096 | tf_op jit(solution)/shard_map/all_to_all | solution.py:78
  8.7 14.6 %all_gather.6 = bf16[2,32,16,128]{3,2,1,0:T(8,128)(2,1)S(1)} all-gather(bf16[2,8,16,128]{3,2,1,0:T(8,128)(2,1)} %param.9), channel_id=1, replica_groups=mesh['parts'=2,'dp'=4,'tensor'=4] {'dp'}, dimensions={1}, use_global_device_ids=true | all-gather | bytes 327680 | tf_op jit(solution)/shard_map/all_gather | solution.py:115
  23.4 2.5 %fusion.38 = (bf16[1,1792,2,128]{3,2,1,0:T(2,128)(2,1)S(1)}, bf16[1,1792,2,128]{3,2,1,0:T(2,128)(2,1)S(1)}) fusion(bf16[2,1792,2,128]{3,2,1,0:T(2,128)(2,1)} %param.7), kind=kLoop, calls=%fused_computation.88 | loop fusion | bytes 3670016 | tf_op jit(solution)/shard_map/slice | solution.py:45
  25.9 4.1 %bitcast_reduce_fusion = (f32[64,2,8]{0,2,1:T(8,128)S(1)}, f32[2,1792,64,8]{1,2,3,0:T(8,128)}) fusion(bf16[64,2,8,128]{3,0,2,1:T(8,128)(2,1)S(1)} %bitcast.113, bf16[1,1792,2,128]{3,2,1,0:T(2,128)(2,1)S(1)} %get-tuple-element.35), kind=kOutput, calls=%fused_computation.4 | convolution fusion | flops 473431040 | bytes 8523776 | tf_op jit(solution)/shard_map/while/body/eval_jaxpr/pcgd,kcd->pcgk/dot_general | solution.py:49
  30.2 4.4 %fusion.3 = f32[2,64,8,128]{3,1,2,0:T(8,128)S(1)} fusion(f32[2,1792,64,8]{1,2,3,0:T(8,128)} %get-tuple-element.48, f32[64,2,8]{0,2,1:T(8,128)S(1)} %get-tuple-element.47, bf16[1,1792,2,128]{3,2,1,0:T(2,128)(2,1)S(1)} %get-tuple-element.34), kind=kOutput, calls=%fused_computation.8 | convolution fusion | flops 475267072 | bytes 8785920 | tf_op jit(solution)/shard_map/while/body/eval_jaxpr/pcgk,kcd->pcgd/dot_general | solution.py:33
  34.6 0.7 reshape.241
  35.3 4.9 %all-to-all-start.1 = ((f32[4,1,256]{2,1,0:T(1,128)}), f32[4,1,256]{2,1,0:T(1,128)S(1)}, u32[]{:S(2)}, u32[]{:S(2)}) async-start(f32[4,1,256]{2,1,0:T(1,128)} %reshape.241), calls=%async_computation.1 | async-start | bytes 8192 | tf_op jit(solution)/shard_map/all_to_all | solution.py:123
  40.2 4.4 %fusion.1 = f32[64,2,8]{0,2,1:T(8,128)S(1)} fusion(f32[2,1792,64,8]{1,2,3,0:T(8,128)} %get-tuple-element.48, f32[64,2,8]{0,2,1:T(8,128)S(1)} %get-tuple-element.47), kind=kLoop, calls=%fused_computation.6 | loop fusion | flops 5504000 | bytes 7348224 | tf_op jit(solution)/shard_map/while/body/eval_jaxpr/reduce_sum | solution.py:36
  44.6 1.1 copy.104
  45.9 0.7 reshape.243
  46.6 5.1 %all-to-all-start.4 = ((f32[4,1,256]{2,1,0:T(1,128)}), f32[4,1,256]{2,1,0:T(1,128)S(1)}, u32[]{:S(2)}, u32[]{:S(2)}) async-start(f32[4,1,256]{2,1,0:T(1,128)} %reshape.243), calls=%async_computation.4 | async-start | bytes 8192 | tf_op jit(solution)/shard_map/all_to_all | solution.py:130
  51.8 5.5 %all-to-all-done.4 = f32[4,1,256]{2,1,0:T(1,128)S(1)} async-done(((f32[4,1,256]{2,1,0:T(1,128)}), f32[4,1,256]{2,1,0:T(1,128)S(1)}, u32[]{:S(2)}, u32[]{:S(2)}) %all-to-all-start.4) | async-done | bytes 4128 | tf_op jit(solution)/shard_map/all_to_all | solution.py:130
  57.3 4.1 %all-to-all-start = ((f32[2,4,8,16,128]{4,3,2,0,1:T(8,128)}), f32[2,4,8,16,128]{4,3,2,0,1:T(8,128)}, u32[]{:S(2)}, u32[]{:S(2)}) async-start(f32[2,4,8,16,128]{4,3,2,0,1:T(8,128)} %copy.104), calls=%async_computation | async-start | bytes 1048576 | tf_op jit(solution)/shard_map/all_to_all | solution.py:137
  61.4 5.1 %gather_fusion = bf16[16,2,128,2,128]{4,3,2,1,0:T(2,128)(2,1)S(1)} fusion(bf16[8,2,128,2,128]{4,3,2,1,0:T(2,128)(2,1)S(1)} %copy-done, s32[1024]{0:T(1024)S(1)} %pad_clamp_fusion.2), kind=kCustom, calls=%fused_computation | custom fusion | bytes 4194368 | tf_op jit(solution)/shard_map/jit(_take)/gather | solution.py:85
  66.5 1.7 %copy_select_fusion = bf16[4,4,2,128,2,128]{5,3,4,2,1,0:T(8,128)(2,1)} fusion(bf16[4,4,2,128,2,128]{5,4,3,2,1,0:T(2,128)(2,1)S(1)} %bitcast.110, pred[4,4]{1,0:T(4,128)(4,1)S(1)} %compare_and_fusion), kind=kLoop, calls=%fused_computation.11 | loop fusion | flops 1048576 | bytes 4194320 | tf_op jit(solution)/shard_map/jit(_take)/select_n | solution.py:85
  68.2 3.7 %all-to-all-done = f32[2,4,8,16,128]{4,3,2,0,1:T(8,128)} async-done(((f32[2,4,8,16,128]{4,3,2,0,1:T(8,128)}), f32[2,4,8,16,128]{4,3,2,0,1:T(8,128)}, u32[]{:S(2)}, u32[]{:S(2)}) %all-to-all-start) | async-done | bytes 524320 | tf_op jit(solution)/shard_map/all_to_all | solution.py:137
  71.9 3.6 %all-to-all-start.3 = ((bf16[4,4,2,128,2,128]{5,3,4,2,1,0:T(8,128)(2,1)}), bf16[4,4,2,128,2,128]{5,3,4,2,1,0:T(8,128)(2,1)S(1)}, u32[]{:S(2)}, u32[]{:S(2)}) async-start(bf16[4,4,2,128,2,128]{5,3,4,2,1,0:T(8,128)(2,1)} %copy_select_fusion), calls=%async_computation.3 | async-start | bytes 4194304 | tf_op jit(solution)/shard_map/all_to_all | solution.py:86
  77.7 31.2 %all-reduce = f32[32]{0:T(128)S(1)} all-reduce(f32[32]{0:T(128)S(1)} %dynamic-update-slice), channel_id=1, replica_groups=mesh['parts'=2,'dp'=4,'tensor'=4] {'dp'}, use_global_device_ids=true, to_apply=%add | all-reduce | flops 32 | bytes 256
  109.7 0.7 reduce.4
  110.4 0.7 reduce.5
  111.2 1.3 multiply_reduce_fusion
  112.5 4.7 %all-to-all-done.3 = bf16[4,4,2,128,2,128]{5,3,4,2,1,0:T(8,128)(2,1)S(1)} async-done(((bf16[4,4,2,128,2,128]{5,3,4,2,1,0:T(8,128)(2,1)}), bf16[4,4,2,128,2,128]{5,3,4,2,1,0:T(8,128)(2,1)S(1)}, u32[]{:S(2)}, u32[]{:S(2)}) %all-to-all-start.3) | async-done | bytes 2097184 | tf_op jit(solution)/shard_map/all_to_all | solution.py:86
  117.2 1.7 %gather_fusion.1 = bf16[8,2,128,2,128]{4,2,3,1,0:T(8,128)(2,1)} fusion(bf16[16,2,128,2,128]{4,2,3,1,0:T(8,128)(2,1)S(1)} %bitcast.111, s32[1024]{0:T(1024)S(1)} %pad_clamp_fusion.1), kind=kCustom, calls=%fused_computation.1 | custom fusion | bytes 2097184 | tf_op jit(solution)/shard_map/jit(_take)/gather | solution.py:87
  118.9 1.4 copy_select_fusion.1
  121.9 0.6 gather_fusion.2
  122.6 5.7 %psum.14 = f32[8]{0:T(128)S(1)} all-reduce(f32[8]{0:T(128)S(1)} %multiply_reduce_fusion.1), channel_id=1, replica_groups=mesh['parts'=2,'dp'=4,'tensor'=4] {'tensor'}, use_global_device_ids=true, to_apply=%region_12.13 | all-reduce | flops 8 | bytes 64 | tf_op jit(solution)/shard_map/psum | solution.py:150
  128.2 0.6 fusion.34
  128.8 16.2 %pmax.7 = f32[]{:T(128)} all-reduce(f32[]{:T(128)} %get-tuple-element.16), channel_id=1, replica_groups=mesh['parts'=2,'dp'=4,'tensor'=4] {'dp'}, use_global_device_ids=true, to_apply=%region_14.15 | all-reduce | flops 1 | bytes 8 | tf_op jit(solution)/shard_map/pmax | solution.py:152
  145.0 1.3 exponential_reduce_fusion
  146.3 9.1 %psum.15 = f32[]{:T(128)} all-reduce(f32[]{:T(128)} %exponential_reduce_fusion), channel_id=1, replica_groups=mesh['parts'=2,'dp'=4,'tensor'=4] {'dp'}, use_global_device_ids=true, to_apply=%region_16.17 | all-reduce | flops 1 | bytes 8 | tf_op jit(solution)/shard_map/psum | solution.py:153
  (64 shorter events, 5.5 us)
Async XLA Ops:
  0.6 60.8 %copy-start = (bf16[8,2,128,2,128]{4,3,2,1,0:T(2,128)(2,1)S(1)}, bf16[8,2,128,2,128]{4,3,2,1,0:T(2,128)(2,1)}, u32[]{:S(2)}) copy-start(bf16[8,2,128,2,128]{4,3,2,1,0:T(2,128)(2,1)} %param.8) | copy-start | bytes 3145732
  2.4 32.9 %all-to-all-start.2 = ((s32[4,1,4]{2,1,0:T(1,128)}), s32[4,1,4]{2,1,0:T(1,128)S(1)}, u32[]{:S(2)}, u32[]{:S(2)}) async-start(s32[4,1,4]{2,1,0:T(1,128)} %bitcast.10), calls=%async_computation.2 | async-start | bytes 4096 | tf_op jit(solution)/shard_map/all_to_all | solution.py:78
  35.3 11.3 %all-to-all-start.1 = ((f32[4,1,256]{2,1,0:T(1,128)}), f32[4,1,256]{2,1,0:T(1,128)S(1)}, u32[]{:S(2)}, u32[]{:S(2)}) async-start(f32[4,1,256]{2,1,0:T(1,128)} %reshape.241), calls=%async_computation.1 | async-start | bytes 8192 | tf_op jit(solution)/shard_map/all_to_all | solution.py:123
  44.6 30.9 %copy-start.3 = (bf16[2,2,8,2,128]{4,3,2,1,0:T(2,128)(2,1)S(1)}, bf16[2,2,8,2,128]{4,3,2,1,0:T(2,128)(2,1)}, u32[]{:S(2)}) copy-start(bf16[2,2,8,2,128]{4,3,2,1,0:T(2,128)(2,1)} %param.10) | copy-start | bytes 49156
  44.6 30.9 %copy-start.2 = (bf16[2,8,16,128]{3,2,1,0:T(8,128)(2,1)S(1)}, bf16[2,8,16,128]{3,2,1,0:T(8,128)(2,1)}, u32[]{:S(2)}) copy-start(bf16[2,8,16,128]{3,2,1,0:T(8,128)(2,1)} %param.9) | copy-start | bytes 196612
  45.7 30.5 %copy-start.7 = (u32[32]{0:T(128)S(1)}, u32[32]{0:T(128)}, u32[]{:S(2)}) copy-start(u32[32]{0:T(128)} %constant.108) | copy-start | bytes 388
  45.7 31.8 %copy-start.6 = (f32[8]{0:T(128)S(1)}, f32[8]{0:T(128)}, u32[]{:S(2)}) copy-start(f32[8]{0:T(128)} %param.12) | copy-start | bytes 100
  46.6 10.7 %all-to-all-start.4 = ((f32[4,1,256]{2,1,0:T(1,128)}), f32[4,1,256]{2,1,0:T(1,128)S(1)}, u32[]{:S(2)}, u32[]{:S(2)}) async-start(f32[4,1,256]{2,1,0:T(1,128)} %reshape.243), calls=%async_computation.4 | async-start | bytes 8192 | tf_op jit(solution)/shard_map/all_to_all | solution.py:130
  57.3 14.6 %all-to-all-start = ((f32[2,4,8,16,128]{4,3,2,0,1:T(8,128)}), f32[2,4,8,16,128]{4,3,2,0,1:T(8,128)}, u32[]{:S(2)}, u32[]{:S(2)}) async-start(f32[2,4,8,16,128]{4,3,2,0,1:T(8,128)} %copy.104), calls=%async_computation | async-start | bytes 1048576 | tf_op jit(solution)/shard_map/all_to_all | solution.py:137
  68.2 53.6 %copy-start.4 = (f32[16,128]{1,0:T(8,128)S(1)}, f32[16,128]{1,0:T(8,128)}, u32[]{:S(2)}) copy-start(f32[16,128]{1,0:T(8,128)} %param.13) | copy-start | bytes 24580
  68.2 60.0 %copy-start.5 = (s32[8]{0:T(128)S(1)}, s32[8]{0:T(128)}, u32[]{:S(2)}) copy-start(s32[8]{0:T(128)} %param.11) | copy-start | bytes 100
  71.9 45.4 %all-to-all-start.3 = ((bf16[4,4,2,128,2,128]{5,3,4,2,1,0:T(8,128)(2,1)}), bf16[4,4,2,128,2,128]{5,3,4,2,1,0:T(8,128)(2,1)S(1)}, u32[]{:S(2)}, u32[]{:S(2)}) async-start(bf16[4,4,2,128,2,128]{5,3,4,2,1,0:T(8,128)(2,1)} %copy_select_fusion), calls=%async_computation.3 | async-start | bytes 4194304 | tf_op jit(solution)/shard_map/all_to_all | solution.py:86
  121.8 35.5 %copy-start.1 = (bf16[2,8,16,128]{3,2,1,0:T(8,128)(2,1)}, bf16[2,8,16,128]{3,2,1,0:T(8,128)(2,1)S(1)}, u32[]{:S(2)}) copy-start(bf16[2,8,16,128]{3,2,1,0:T(8,128)(2,1)S(1)} %fusion.13) | copy-start | bytes 196612
where the time goes:
time: 158 us; the launch traced here: 157 us
  blocking collectives  76.7 us (49%)
  starting transfers between devices  24 us (15%)
  local copies, waits for them, and re-layouts  15.4 us (10%)
  other arithmetic  14.3 us (9%)
  waiting for transfers between devices  13.9 us (9%)
  matrix products  9.94 us (6%)
  between operations  2.94 us (2%)
    unnamed x1, blocking collectives  31.2 us
    pmax x1, blocking collectives, per_device(): largest_weight = lax.pmax(jnp.max(raw_weight), 'dp')  16.2 us
    all_gather x1, blocking collectives, per_device(): everyone = lax.all_gather(queries, 'dp', axis=1, tiled=True)  14.6 us
    psum x1, blocking collectives, per_device(): weight_mass = lax.psum(jnp.sum(jnp.exp(raw_weight - largest_weight)), 'dp')  9.05 us
    all_to_all x1, starting transfers between devices, per_device(): lax.all_to_all(wanted.reshape(devices, capacity), 'dp', split_axis=0, con...  6.35 us
    psum x1, blocking collectives, per_device(): twist_value = lax.psum(local_twist, 'tensor')  5.66 us
    all_to_all x1, waiting for transfers between devices, per_device(): lax.all_to_all(totals.reshape(step_count, devices, local_count, head_coun...  5.47 us
    all_to_all x1, starting transfers between devices, per_device(): lax.all_to_all(totals.reshape(step_count, devices, local_count, head_coun...  5.09 us
  transfers between devices with their start and end apart: 5, of which 3 were waited for; matrix products, arithmetic and copies ran while one was open for 19% of the time, Pallas kernels for 0%

commit v1 on v0

v1 whole, which is shorter than its diff:
```python
import functools
import math

import jax
import jax.numpy as jnp
from jax import lax
from jax.experimental import pallas as pl
from jax.experimental.pallas import tpu as pltpu
from jax.sharding import PartitionSpec as P

MESH = pl.DeviceIdType.MESH
MASKED = -1e30
LEVELS = 32767.0


def nt(a, b):
    return lax.dot_general(a, b, (((1,), (1,)), ((), ())), preferred_element_type=jnp.float32)


def tn_dot(a, b):
    return lax.dot_general(a, b, (((0,), (0,)), ((), ())), preferred_element_type=jnp.float32)


def kernel(
    sizes,
    anc_ref,
    prior_ref,
    vec_ref,
    new_ref,
    q_hbm,
    prompt_hbm,
    gen_hbm,
    att_ref,
    lw_ref,
    prompt_buf,
    gen_buf,
    wide,
    keys,
    vals,
    gkeys,
    gvals,
    q_all,
    meta_own,
    meta_all,
    res_send,
    res_recv,
    stat_send,
    stat_recv,
    tens_own,
    tens_all,
    dp_own,
    dp_all,
    local_sem,
    q_ssem,
    q_rsem,
    m_ssem,
    m_rsem,
    r_ssem,
    r_rsem,
    s_ssem,
    s_rsem,
    t_ssem,
    t_rsem,
    d_ssem,
    d_rsem,
):
    devices, tensors, steps, local, kv_count, group, positions, cached, head = sizes
    rows = steps * local * group
    all_heads = kv_count * group
    me = lax.axis_index("dp")
    mine = lax.axis_index("tensor")
    factor = math.log2(math.e) / math.sqrt(head)

    def remote(src, dst, ssem, rsem, **where):
        return pltpu.make_async_remote_copy(
            src_ref=src, dst_ref=dst, send_sem=ssem, recv_sem=rsem,
            device_id=where, device_id_type=MESH,
        )

    barrier = pltpu.get_barrier_semaphore()

    @pl.loop(1, devices)
    def _(k):
        pl.semaphore_signal(
            barrier, inc=1, device_id={"dp": lax.rem(me + k, devices)}, device_id_type=MESH
        )

    @pl.loop(1, tensors)
    def _(k):
        pl.semaphore_signal(
            barrier, inc=1, device_id={"tensor": lax.rem(mine + k, tensors)}, device_id_type=MESH
        )

    copy_q = pltpu.make_async_copy(q_hbm, q_all.at[me], local_sem.at[0])
    copy_q.start()
    copy_k = pltpu.make_async_copy(prompt_hbm.at[0], prompt_buf.at[0], local_sem.at[1])
    copy_k.start()
    copy_v = pltpu.make_async_copy(prompt_hbm.at[1], prompt_buf.at[1], local_sem.at[2])
    copy_v.start()
    copy_g = pltpu.make_async_copy(gen_hbm, gen_buf, local_sem.at[3])
    copy_g.start()

    lane = lax.broadcasted_iota(jnp.int32, (8, rows), 1)
    sub = lax.broadcasted_iota(jnp.int32, (8, rows), 0)
    lane_particle = lax.rem(lax.div(lane, group), local)
    meta = jnp.zeros((8, rows), jnp.float32)
    for j in range(local):
        meta = jnp.where(
            (sub == 0) & (lane_particle == j), anc_ref[j].astype(jnp.float32), meta
        )
        meta = jnp.where((sub == 1) & (lane == j), prior_ref[j], meta)
    meta_own[...] = meta
    meta_all[me] = meta

    pl.semaphore_wait(barrier, devices - 1 + tensors - 1)

    def q_copy(peer, slot):
        return remote(q_hbm, q_all.at[slot], q_ssem.at[peer], q_rsem.at[slot], dp=peer)

    def m_copy(peer, slot):
        return remote(meta_own, meta_all.at[slot], m_ssem.at[peer], m_rsem.at[slot], dp=peer)

    def r_copy(peer, slot):
        return remote(res_send.at[peer], res_recv.at[slot], r_ssem.at[peer], r_rsem.at[slot], dp=peer)

    def s_copy(peer, slot):
        return remote(stat_send.at[peer], stat_recv.at[slot], s_ssem.at[peer], s_rsem.at[slot], dp=peer)

    @pl.loop(1, devices)
    def _(k):
        peer = lax.rem(me + k, devices)
        m_copy(peer, me).start()
        q_copy(peer, me).start()

    def split(source, count):
        wide[pl.ds(0, count * kv_count), :] = source.astype(jnp.float32)
        return [
            wide[pl.ds(c, count, stride=kv_count), :] if kv_count > 1 else wide[pl.ds(0, count), :]
            for c in range(kv_count)
        ]

    chunk = cached

    copy_k.wait()

    @pl.loop(0, positions // chunk)
    def _(i):
        at = pl.ds(pl.multiple_of(i * (chunk * kv_count), chunk * kv_count), chunk * kv_count)
        for c, part in enumerate(split(prompt_buf[0, at, :], chunk)):
            keys[c, pl.ds(pl.multiple_of(i * chunk, chunk), chunk), :] = part.astype(jnp.bfloat16)

    copy_v.wait()

    @pl.loop(0, positions // chunk)
    def _(i):
        at = pl.ds(pl.multiple_of(i * (chunk * kv_count), chunk * kv_count), chunk * kv_count)
        for c, part in enumerate(split(prompt_buf[1, at, :], chunk)):
            vals[c, :, pl.ds(pl.multiple_of(i * chunk, chunk), chunk)] = part.T.astype(jnp.bfloat16)

    copy_g.wait()

    @pl.loop(0, local)
    def _(i):
        at = pl.ds(pl.multiple_of(i * chunk, chunk), chunk)
        for c, part in enumerate(split(gen_buf[i, 0], chunk)):
            gkeys[c, at, :] = part.astype(jnp.bfloat16)
        for c, part in enumerate(split(gen_buf[i, 1], chunk)):
            gvals[c, :, at] = part.T.astype(jnp.bfloat16)

    def rows_of(slot, c):
        q = q_all[slot].astype(jnp.float32).reshape(steps * local, kv_count, group, head)
        return q[:, c].reshape(rows, head).astype(jnp.bfloat16)

    def partial(slot, res, stat):
        ancestor = meta_all[slot, 0:1, :]
        held = (ancestor - (me * local).astype(jnp.float32)).astype(jnp.int32)
        for c in range(kv_count):
            q = rows_of(slot, c)
            score = nt(keys[c], q)
            top = jnp.max(score, axis=0, keepdims=True)
            weight = jnp.exp2((score - top) * factor)
            total = jnp.sum(weight, axis=0, keepdims=True)
            value = jnp.dot(vals[c], weight.astype(jnp.bfloat16), preferred_element_type=jnp.float32)
            gscore = nt(gkeys[c], q).reshape(local, cached, rows)
            which = lax.broadcasted_iota(jnp.int32, (local, 1, rows), 0)
            gscore = jnp.where(which == held[None], gscore, MASKED).reshape(local * cached, rows)
            gtop = jnp.max(gscore, axis=0, keepdims=True)
            gweight = jnp.exp2((gscore - gtop) * factor)
            gtotal = jnp.sum(gweight, axis=0, keepdims=True)
            gvalue = jnp.dot(gvals[c], gweight.astype(jnp.bfloat16), preferred_element_type=jnp.float32)
            both = jnp.maximum(top, gtop)
            one = jnp.exp2((top - both) * factor)
            two = jnp.exp2((gtop - both) * factor)
            value = value * one + gvalue * two
            total = total * one + gtotal * two
            largest = jnp.maximum(jnp.max(jnp.abs(value), axis=0, keepdims=True), 1e-30)
            coded = value * (LEVELS / largest)
            coded = coded + jnp.where(coded >= 0, 0.5, -0.5)
            res[c] = coded.astype(jnp.int32).astype(jnp.int16)
            stat[c, 0:1, :] = both
            stat[c, 1:2, :] = total
            stat[c, 2:3, :] = largest * (1.0 / LEVELS)

    copy_q.wait()
    partial(me, res_recv.at[me], stat_recv.at[me])

    @pl.loop(1, devices)
    def _(k):
        peer = lax.rem(me + devices - k, devices)
        m_copy(peer, peer).wait_recv()
        q_copy(peer, peer).wait_recv()
        partial(peer, res_send.at[peer], stat_send.at[peer])
        s_copy(peer, me).start()
        r_copy(peer, me).start()

    fresh_keys = jnp.concatenate(
        [new_ref[t, 0].astype(jnp.float32) for t in range(steps)], axis=0
    ).astype(jnp.bfloat16)
    fresh_vals = jnp.concatenate(
        [new_ref[t, 1].astype(jnp.float32) for t in range(steps)], axis=0
    ).astype(jnp.bfloat16)
    count = steps * local * kv_count
    key_place = lax.broadcasted_iota(jnp.int32, (count, rows), 0)
    row_place = lax.broadcasted_iota(jnp.int32, (count, rows), 1)
    key_head = lax.rem(key_place, kv_count)
    key_particle = lax.rem(lax.div(key_place, kv_count), local)
    key_step = lax.div(key_place, kv_count * local)
    row_particle = lax.rem(lax.div(row_place, group), local)
    row_step = lax.div(row_place, group * local)
    fits = (key_particle == row_particle) & (key_step <= row_step)
    fresh = []
    for c in range(kv_count):
        score = jnp.where(fits & (key_head == c), nt(fresh_keys, rows_of(me, c)), MASKED)
        top = jnp.max(score, axis=0, keepdims=True)
        weight = jnp.exp2((score - top) * factor)
        total = jnp.sum(weight, axis=0, keepdims=True)
        fresh.append((top, total, tn_dot(fresh_vals, weight.astype(jnp.bfloat16))))

    lane8 = lax.broadcasted_iota(jnp.int32, (local, head), 1)
    sub8 = lax.broadcasted_iota(jnp.int32, (local, head), 0)
    own_ancestor = jnp.zeros((local, head), jnp.int32)
    for j in range(local):
        own_ancestor = jnp.where(sub8 == j, anc_ref[j], own_ancestor)

    def add_before(i, before):
        prior = meta_all[i, 1:2, :]
        hit = (own_ancestor - i * local == lane8) & (lane8 < local)
        return before + jnp.where(hit, prior, 0.0)

    before = lax.fori_loop(0, devices, add_before, jnp.zeros((local, head), jnp.float32))
    before = before * (mine == 0).astype(jnp.float32)

    @pl.loop(1, devices)
    def _(k):
        peer = lax.rem(me + devices - k, devices)
        s_copy(peer, peer).wait_recv()
        r_copy(peer, peer).wait_recv()

    outs = []
    for c in range(kv_count):
        top, total, value = fresh[c]

        def join(i, state):
            top, total, value = state
            other = stat_recv[i, c, 0:1, :]
            both = jnp.maximum(top, other)
            one = jnp.exp2((top - both) * factor)
            two = jnp.exp2((other - both) * factor)
            arrived = res_recv[i, c].astype(jnp.int32).astype(jnp.float32)
            return (
                both,
                total * one + stat_recv[i, c, 1:2, :] * two,
                value * one + arrived * (stat_recv[i, c, 2:3, :] * two),
            )

        if devices <= 4:
            state = (top, total, value)
            for i in range(devices):
                state = join(i, state)
        else:
            state = lax.fori_loop(0, devices, join, (top, total, value))
        outs.append((state[2] / state[1]).T.reshape(steps * local, 1, group, head))
    attended = jnp.concatenate(outs, axis=1) if kv_count > 1 else outs[0]
    attended = attended.reshape(steps * local * all_heads, head).astype(jnp.bfloat16)
    att_ref[...] = attended
    last = att_ref[pl.ds((steps - 1) * local * all_heads, local * all_heads), :].astype(jnp.float32)
    last = last.reshape(local, all_heads, head) * vec_ref[...][None]
    twist = jnp.sum(last, axis=1) - before
    tens_own[...] = twist
    tens_all[mine] = twist

    def t_copy(peer, slot):
        return remote(tens_own, tens_all.at[slot], t_ssem.at[peer], t_rsem.at[slot], tensor=peer)

    def d_copy(peer, slot):
        return remote(dp_own, dp_all.at[slot], d_ssem.at[peer], d_rsem.at[slot], dp=peer)

    @pl.loop(1, tensors)
    def _(k):
        t_copy(lax.rem(mine + k, tensors), mine).start()

    @pl.loop(1, tensors)
    def _(k):
        peer = lax.rem(mine + k, tensors)
        t_copy(peer, peer).wait_recv()

    raw = jnp.sum(tens_all[...], axis=0)
    raw = jnp.broadcast_to(jnp.sum(raw, axis=1, keepdims=True), (local, head))
    dp_own[...] = raw
    dp_all[me] = raw

    @pl.loop(1, devices)
    def _(k):
        d_copy(lax.rem(me + k, devices), me).start()

    @pl.loop(1, devices)
    def _(k):
        peer = lax.rem(me + k, devices)
        d_copy(peer, peer).wait_recv()

    every = dp_all[...]
    largest = jnp.max(jnp.max(every, axis=0), axis=0, keepdims=True)
    mass = jnp.sum(jnp.sum(jnp.exp(every - largest[None]), axis=0), axis=0, keepdims=True)
    logs = raw - (largest + jnp.log(mass))
    flat = jnp.sum(jnp.where(sub8 == lane8, logs, 0.0), axis=0, keepdims=True)
    lw_ref[...] = flat[:, :local]

    @pl.loop(1, devices)
    def _(k):
        peer = lax.rem(me + k, devices)
        m_copy(peer, me).wait_send()
        q_copy(peer, me).wait_send()
        s_copy(peer, me).wait_send()
        r_copy(peer, me).wait_send()
        d_copy(peer, me).wait_send()

    @pl.loop(1, tensors)
    def _(k):
        t_copy(lax.rem(mine + k, tensors), mine).wait_send()


def per_device(devices, tensors, prompt_kv, gen_kv, queries, new_kv, ancestors, prior_twist, twist_vec):
    steps, local, heads, head = queries.shape
    kv_count = prompt_kv.shape[2]
    group = heads // kv_count
    positions = prompt_kv.shape[1]
    cached = gen_kv.shape[2]
    rows = steps * local * group
    sizes = (devices, tensors, steps, local, kv_count, group, positions, cached, head)
    bf16, f32 = jnp.bfloat16, jnp.float32
    vmem = pl.BlockSpec(memory_space=pltpu.VMEM)
    smem = pl.BlockSpec(memory_space=pltpu.SMEM)
    hbm = pl.BlockSpec(memory_space=pl.ANY)
    dma = pltpu.SemaphoreType.DMA
    attended, log_weights = pl.pallas_call(
        functools.partial(kernel, sizes),
        name="decode",
        out_shape=(
            jax.ShapeDtypeStruct((steps * local * heads, head), bf16),
            jax.ShapeDtypeStruct((1, local), f32),
        ),
        in_specs=[smem, smem, vmem, vmem, hbm, hbm, hbm],
        out_specs=(vmem, vmem),
        scratch_shapes=[
            pltpu.VMEM((2, positions * kv_count, head), bf16),
            pltpu.VMEM((local, 2, cached * kv_count, head), bf16),
            pltpu.VMEM((cached * kv_count, head), f32),
            pltpu.VMEM((kv_count, positions, head), bf16),
            pltpu.VMEM((kv_count, head, positions), bf16),
            pltpu.VMEM((kv_count, local * cached, head), bf16),
            pltpu.VMEM((kv_count, head, local * cached), bf16),
            pltpu.VMEM((devices, steps * local * heads, head), bf16),
            pltpu.VMEM((8, rows), f32),
            pltpu.VMEM((devices, 8, rows), f32),
            pltpu.VMEM((devices, kv_count, head, rows), jnp.int16),
            pltpu.VMEM((devices, kv_count, head, rows), jnp.int16),
            pltpu.VMEM((devices, kv_count, 8, rows), f32),
            pltpu.VMEM((devices, kv_count, 8, rows), f32),
            pltpu.VMEM((local, head), f32),
            pltpu.VMEM((tensors, local, head), f32),
            pltpu.VMEM((local, head), f32),
            pltpu.VMEM((devices, local, head), f32),
            dma((4,)),
        ]
        + [dma((devices,))] * 8
        + [dma((tensors,))] * 2
        + [dma((devices,))] * 2,
        compiler_params=pltpu.CompilerParams(
            collective_id=0, has_side_effects=True, vmem_limit_bytes=56 * 1024 * 1024
        ),
    )(
        ancestors,
        prior_twist,
        twist_vec,
        new_kv.reshape(steps, 2, local * kv_count, head),
        queries.reshape(steps * local * heads, head),
        prompt_kv.reshape(2, positions * kv_count, head),
        gen_kv.reshape(local, 2, cached * kv_count, head),
    )
    return (attended.reshape(queries.shape), log_weights.reshape(local))


def solution(mesh):
    placed = (
        P(None, ("parts", "dp"), "tensor", None),
        P(("parts", "dp"), None, None, "tensor", None),
        P(None, ("parts", "dp"), "tensor", None),
        P(None, None, ("parts", "dp"), "tensor", None),
        P(("parts", "dp")),
        P(("parts", "dp")),
        P("tensor", None),
    )
    return jax.shard_map(
        functools.partial(per_device, mesh.shape["dp"], mesh.shape["tensor"]),
        mesh=mesh,
        in_specs=placed,
        out_specs=(P(None, ("parts", "dp"), "tensor", None), P(("parts", "dp"))),
        check_vma=False,
    )
```

time: 158 us -> 31.9 us (0.20)
  blocking collectives: 76.7 us -> 0 us
  Pallas kernels: 0 us -> 28.4 us
  starting transfers between devices: 24 us -> 0 us
  other arithmetic: 14.3 us -> 0 us
  waiting for transfers between devices: 13.9 us -> 0 us
  local copies, waits for them, and re-layouts: 15.4 us -> 2.59 us
  matrix products: 9.94 us -> 0 us
  between operations: 2.94 us -> 0.64 us
    unnamed x1 -> x0, blocking collectives: 31.2 us -> none
    pallas_call x0 -> x1, Pallas kernels: none -> 28.4 us  [per_device(): pl.pallas_call(functools.partial(kernel, sizes), name='decode', out_shape...]
    all_to_all x5 -> x0, starting transfers between devices: 24 us -> none  [the longest x1 6.35 us: per_device(): lax.all_to_all(wanted.reshape(devices, capacity), 'dp', split_axis=0, con...]
    pmax x1 -> x0, blocking collectives: 16.2 us -> none  [per_device(): largest_weight = lax.pmax(jnp.max(raw_weight), 'dp')]
    psum x2 -> x0, blocking collectives: 14.7 us -> none  [the longest x1 9.05 us: per_device(): weight_mass = lax.psum(jnp.sum(jnp.exp(raw_weight - largest_weight)), 'dp')]
    all_gather x1 -> x0, blocking collectives: 14.6 us -> none  [per_device(): everyone = lax.all_gather(queries, 'dp', axis=1, tiled=True)]
    all_to_all x5 -> x0, waiting for transfers between devices: 13.9 us -> none  [the longest x1 5.47 us: per_device(): lax.all_to_all(totals.reshape(step_count, devices, local_count, head_coun...]
    dot_general x6 -> x0, matrix products: 9.94 us -> none  [the longest x3 4.96 us: block_state(): jnp.einsum(pattern, exponent.astype(jnp.bfloat16), values, preferred_elem...]
  transfers between devices with their start and end apart: 5 -> 0, of which waited for: 3 -> 0; matrix products, arithmetic and copies ran while one was open for 19% -> 0% of each run, Pallas kernels for 0% -> 0%
where the time goes in v1:
time: 31.9 us; the launch traced here: 31.6 us
  Pallas kernels  28.4 us (89%)
  local copies, waits for them, and re-layouts  2.59 us (8%)
  between operations  0.64 us (2%)
    pallas_call x1, Pallas kernels, per_device(): pl.pallas_call(functools.partial(kernel, sizes), name='decode', out_shape...  28.4 us
    unnamed x2, local copies, waits for them, and re-layouts  2.59 us

profile of v1, /device:TPU:0, one launch (start us, length us, event | category | flops | bytes accessed | tf_op | source)
XLA Modules:
  0.0 31.6 jit_solution(12656094861332379385)
XLA Ops:
  0.6 28.4 %decode.1 = (bf16[256,128]{1,0:T(8,128)(2,1)}, f32[1,8]{1,0:T(1,128)}) custom-call(s32[8]{0:T(128)} %anc_ref.1, f32[8]{0:T(128)} %prior_ref.1, f32[16,128]{1,0:T(8,128)} %vec_ref.1, bf16[2,2,16,128]{3,2,1,0:T(8,128)(2,1)} %bitcast.10, bf16[256,128]{1,0:T(8,128)(2,1)} %bitcast.8, bf16[2,3584,128]{2,1,0:T(8,128)(2,1)} %bitcast.6, bf16[8,2,256,128]{3,2,1,0:T(8,128)(2,1)} %bitcast.7), custom_call_target="tpu_custom_call" | custom-call | tf_op jit(solution)/shard_map/decode/pallas_call | solution.py:355
  29.0 1.5 %copy.11 = bf16[2,8,16,128]{3,2,1,0:T(8,128)(2,1)} copy(bf16[2,8,16,128]{3,2,1,0:T(8,128)(2,1)} %bitcast.9) | data formatting | bytes 131072
  30.5 1.1 %copy.12 = f32[8]{0:T(128)} copy(f32[8]{0:T(128)} %bitcast.11) | data formatting | bytes 64

commit v2 on v1

--- a/solution.py
+++ b/solution.py
@@ -11,6 +11,7 @@
 MESH = pl.DeviceIdType.MESH
 MASKED = -1e30
 LEVELS = 32767.0
+LOWEST = -3e38
 
 
 def nt(a, b):
@@ -23,15 +24,19 @@
 
 def kernel(
     sizes,
-    anc_ref,
-    prior_ref,
-    vec_ref,
-    new_ref,
+    anc_hbm,
+    prior_hbm,
+    vec_hbm,
+    new_hbm,
     q_hbm,
     prompt_hbm,
     gen_hbm,
     att_ref,
     lw_ref,
+    anc_ref,
+    prior_ref,
+    vec_ref,
+    new_ref,
     prompt_buf,
     gen_buf,
     wide,
@@ -46,10 +51,8 @@
     res_recv,
     stat_send,
     stat_recv,
-    tens_own,
-    tens_all,
-    dp_own,
-    dp_all,
+    twist_own,
+    twist_all,
     local_sem,
     q_ssem,
     q_rsem,
@@ -61,8 +64,6 @@
     s_rsem,
     t_ssem,
     t_rsem,
-    d_ssem,
-    d_rsem,
 ):
     devices, tensors, steps, local, kv_count, group, positions, cached, head = sizes
     rows = steps * local * group
@@ -91,6 +92,14 @@
             barrier, inc=1, device_id={"tensor": lax.rem(mine + k, tensors)}, device_id_type=MESH
         )
 
+    small = [
+        pltpu.make_async_copy(src, dst, local_sem.at[4 + i])
+        for i, (src, dst) in enumerate(
+            [(anc_hbm, anc_ref), (prior_hbm, prior_ref), (vec_hbm, vec_ref), (new_hbm, new_ref)]
+        )
+    ]
+    for copy in small:
+        copy.start()
     copy_q = pltpu.make_async_copy(q_hbm, q_all.at[me], local_sem.at[0])
     copy_q.start()
     copy_k = pltpu.make_async_copy(prompt_hbm.at[0], prompt_buf.at[0], local_sem.at[1])
@@ -103,6 +112,8 @@
     lane = lax.broadcasted_iota(jnp.int32, (8, rows), 1)
     sub = lax.broadcasted_iota(jnp.int32, (8, rows), 0)
     lane_particle = lax.rem(lax.div(lane, group), local)
+    small[0].wait()
+    small[1].wait()
     meta = jnp.zeros((8, rows), jnp.float32)
     for j in range(local):
         meta = jnp.where(
@@ -197,9 +208,9 @@
             coded = value * (LEVELS / largest)
             coded = coded + jnp.where(coded >= 0, 0.5, -0.5)
             res[c] = coded.astype(jnp.int32).astype(jnp.int16)
-            stat[c, 0:1, :] = both
-            stat[c, 1:2, :] = total
-            stat[c, 2:3, :] = largest * (1.0 / LEVELS)
+            stat[3 * c : 3 * c + 1, :] = both
+            stat[3 * c + 1 : 3 * c + 2, :] = total
+            stat[3 * c + 2 : 3 * c + 3, :] = largest * (1.0 / LEVELS)
 
     copy_q.wait()
     partial(me, res_recv.at[me], stat_recv.at[me])
@@ -212,6 +223,9 @@
         partial(peer, res_send.at[peer], stat_send.at[peer])
         s_copy(peer, me).start()
         r_copy(peer, me).start()
+
+    small[2].wait()
+    small[3].wait()
 
     fresh_keys = jnp.concatenate(
         [new_ref[t, 0].astype(jnp.float32) for t in range(steps)], axis=0
@@ -262,15 +276,15 @@
 
         def join(i, state):
             top, total, value = state
-            other = stat_recv[i, c, 0:1, :]
+            other = stat_recv[i, 3 * c : 3 * c + 1, :]
             both = jnp.maximum(top, other)
             one = jnp.exp2((top - both) * factor)
             two = jnp.exp2((other - both) * factor)
             arrived = res_recv[i, c].astype(jnp.int32).astype(jnp.float32)
             return (
                 both,
-                total * one + stat_recv[i, c, 1:2, :] * two,
-                value * one + arrived * (stat_recv[i, c, 2:3, :] * two),
+                total * one + stat_recv[i, 3 * c + 1 : 3 * c + 2, :] * two,
+                value * one + arrived * (stat_recv[i, 3 * c + 2 : 3 * c + 3, :] * two),
             )
 
         if devices <= 4:
@@ -286,44 +300,44 @@
     last = att_ref[pl.ds((steps - 1) * local * all_heads, local * all_heads), :].astype(jnp.float32)
     last = last.reshape(local, all_heads, head) * vec_ref[...][None]
     twist = jnp.sum(last, axis=1) - before
-    tens_own[...] = twist
-    tens_all[mine] = twist
-
-    def t_copy(peer, slot):
-        return remote(tens_own, tens_all.at[slot], t_ssem.at[peer], t_rsem.at[slot], tensor=peer)
-
-    def d_copy(peer, slot):
-        return remote(dp_own, dp_all.at[slot], d_ssem.at[peer], d_rsem.at[slot], dp=peer)
-
-    @pl.loop(1, tensors)
-    def _(k):
-        t_copy(lax.rem(mine + k, tensors), mine).start()
-
-    @pl.loop(1, tensors)
-    def _(k):
-        peer = lax.rem(mine + k, tensors)
-        t_copy(peer, peer).wait_recv()
-
-    raw = jnp.sum(tens_all[...], axis=0)
-    raw = jnp.broadcast_to(jnp.sum(raw, axis=1, keepdims=True), (local, head))
-    dp_own[...] = raw
-    dp_all[me] = raw
-
-    @pl.loop(1, devices)
-    def _(k):
-        d_copy(lax.rem(me + k, devices), me).start()
-
-    @pl.loop(1, devices)
-    def _(k):
-        peer = lax.rem(me + k, devices)
-        d_copy(peer, peer).wait_recv()
-
-    every = dp_all[...]
-    largest = jnp.max(jnp.max(every, axis=0), axis=0, keepdims=True)
-    mass = jnp.sum(jnp.sum(jnp.exp(every - largest[None]), axis=0), axis=0, keepdims=True)
-    logs = raw - (largest + jnp.log(mass))
-    flat = jnp.sum(jnp.where(sub8 == lane8, logs, 0.0), axis=0, keepdims=True)
-    lw_ref[...] = flat[:, :local]
+    column = jnp.sum(twist, axis=1, keepdims=True)
+    flat = jnp.sum(jnp.where(sub8 == lane8, column, 0.0), axis=0, keepdims=True)
+    place = me * tensors + mine
+    everyone = devices * tensors
+    twist_own[...] = flat
+    twist_all[place] = flat
+
+    def t_copy(k, slot):
+        peer = lax.rem(place + k, everyone)
+        where = dict(dp=lax.div(peer, tensors), tensor=lax.rem(peer, tensors))
+        slot = place if slot is None else peer
+        return remote(twist_own, twist_all.at[slot], t_ssem.at[peer], t_rsem.at[slot], **where)
+
+    @pl.loop(1, everyone)
+    def _(k):
+        t_copy(k, None).start()
+
+    @pl.loop(1, everyone)
+    def _(k):
+        t_copy(k, k).wait_recv()
+
+    def of_device(i):
+        return jnp.sum(twist_all[pl.ds(i * tensors, tensors)], axis=0)
+
+    real = lax.broadcasted_iota(jnp.int32, (1, head), 1) < local
+
+    def larger(i, top):
+        return jnp.maximum(top, jnp.where(real, of_device(i), LOWEST))
+
+    def heavier(i, mass):
+        return mass + jnp.where(real, jnp.exp(of_device(i) - largest), 0.0)
+
+    largest = lax.fori_loop(0, devices, larger, jnp.full((1, head), LOWEST), unroll=devices <= 4)
+    largest = jnp.max(largest, axis=1, keepdims=True)
+    mass = lax.fori_loop(0, devices, heavier, jnp.zeros((1, head)), unroll=devices <= 4)
+    mass = jnp.sum(mass, axis=1, keepdims=True)
+    logs = of_device(me) - (largest + jnp.log(mass))
+    lw_ref[...] = logs[:, :local]
 
     @pl.loop(1, devices)
     def _(k):
@@ -332,11 +346,21 @@
         q_copy(peer, me).wait_send()
         s_copy(peer, me).wait_send()
         r_copy(peer, me).wait_send()
-        d_copy(peer, me).wait_send()
-
-    @pl.loop(1, tensors)
-    def _(k):
-        t_copy(lax.rem(mine + k, tensors), mine).wait_send()
+
+    @pl.loop(1, everyone)
+    def _(k):
+        t_copy(k, None).wait_send()
+
+
+def write_out(att_ref, lw_ref, att_out, lw_out, sems):
+    copies = [
+        pltpu.make_async_copy(att_ref, att_out, sems.at[0]),
+        pltpu.make_async_copy(lw_ref, lw_out, sems.at[1]),
+    ]
+    for copy in copies:
+        copy.start()
+    for copy in copies:
+        copy.wait()
 
 
 def per_device(devices, tensors, prompt_kv, gen_kv, queries, new_kv, ancestors, prior_twist, twist_vec):
@@ -346,22 +370,26 @@
     positions = prompt_kv.shape[1]
     cached = gen_kv.shape[2]
     rows = steps * local * group
+    stats = 8 * pl.cdiv(3 * kv_count, 8)
     sizes = (devices, tensors, steps, local, kv_count, group, positions, cached, head)
     bf16, f32 = jnp.bfloat16, jnp.float32
     vmem = pl.BlockSpec(memory_space=pltpu.VMEM)
-    smem = pl.BlockSpec(memory_space=pltpu.SMEM)
     hbm = pl.BlockSpec(memory_space=pl.ANY)
     dma = pltpu.SemaphoreType.DMA
     attended, log_weights = pl.pallas_call(
         functools.partial(kernel, sizes),
         name="decode",
         out_shape=(
-            jax.ShapeDtypeStruct((steps * local * heads, head), bf16),
-            jax.ShapeDtypeStruct((1, local), f32),
+            pltpu.VMEM((steps * local * heads, head), bf16),
+            pltpu.VMEM((1, local), f32),
         ),
-        in_specs=[smem, smem, vmem, vmem, hbm, hbm, hbm],
+        in_specs=[hbm] * 7,
         out_specs=(vmem, vmem),
         scratch_shapes=[
+            pltpu.SMEM((local,), jnp.int32),
+            pltpu.SMEM((local,), f32),
+            pltpu.VMEM((heads, head), f32),
+            pltpu.VMEM((steps, 2, local * kv_count, head), bf16),
             pltpu.VMEM((2, positions * kv_count, head), bf16),
             pltpu.VMEM((local, 2, cached * kv_count, head), bf16),
             pltpu.VMEM((cached * kv_count, head), f32),
@@ -374,17 +402,14 @@
             pltpu.VMEM((devices, 8, rows), f32),
             pltpu.VMEM((devices, kv_count, head, rows), jnp.int16),
             pltpu.VMEM((devices, kv_count, head, rows), jnp.int16),
-            pltpu.VMEM((devices, kv_count, 8, rows), f32),
-            pltpu.VMEM((devices, kv_count, 8, rows), f32),
-            pltpu.VMEM((local, head), f32),
-            pltpu.VMEM((tensors, local, head), f32),
-            pltpu.VMEM((local, head), f32),
-            pltpu.VMEM((devices, local, head), f32),
-            dma((4,)),
+            pltpu.VMEM((devices, stats, rows), f32),
+            pltpu.VMEM((devices, stats, rows), f32),
+            pltpu.VMEM((1, head), f32),
+            pltpu.VMEM((devices * tensors, 1, head), f32),
+            dma((8,)),
         ]
         + [dma((devices,))] * 8
-        + [dma((tensors,))] * 2
-        + [dma((devices,))] * 2,
+        + [dma((devices * tensors,))] * 2,
         compiler_params=pltpu.CompilerParams(
             collective_id=0, has_side_effects=True, vmem_limit_bytes=56 * 1024 * 1024
         ),
@@ -397,6 +422,17 @@
         prompt_kv.reshape(2, positions * kv_count, head),
         gen_kv.reshape(local, 2, cached * kv_count, head),
     )
+    attended, log_weights = pl.pallas_call(
+        write_out,
+        name="write_out",
+        out_shape=(
+            jax.ShapeDtypeStruct((steps * local * heads, head), bf16),
+            jax.ShapeDtypeStruct((1, local), f32),
+        ),
+        in_specs=[vmem, vmem],
+        out_specs=(hbm, hbm),
+        scratch_shapes=[dma((2,))],
+    )(pltpu.with_memory_space_constraint(attended, pltpu.VMEM), pltpu.with_memory_space_constraint(log_weights, pltpu.VMEM))
     return (attended.reshape(queries.shape), log_weights.reshape(local))
 
 

time: 31.9 us -> 26.5 us (0.83)
  Pallas kernels: 28.4 us -> 25.7 us
  local copies, waits for them, and re-layouts: 2.59 us -> 0 us
    pallas_call x1, Pallas kernels: 28.4 us -> 25.1 us  [per_device(): pl.pallas_call(functools.partial(kernel, sizes), name='decode', out_shape...]
    unnamed x2 -> x0, local copies, waits for them, and re-layouts: 2.59 us -> none
    pallas_call x0 -> x1, Pallas kernels: none -> 0.65 us  [per_device(): pl.pallas_call(write_out, name='write_out', out_shape=(jax.ShapeDtypeStru...]
where the time goes in v2:
time: 26.5 us; the launch traced here: 26.3 us
  Pallas kernels  25.7 us (97%)
  between operations  0.64 us (2%)
    pallas_call x1, Pallas kernels, per_device(): pl.pallas_call(functools.partial(kernel, sizes), name='decode', out_shape...  25.1 us
    pallas_call x1, Pallas kernels, per_device(): pl.pallas_call(write_out, name='write_out', out_shape=(jax.ShapeDtypeStru...  0.65 us

profile of v2, /device:TPU:0, one launch (start us, length us, event | category | flops | bytes accessed | tf_op | source)
XLA Modules:
  0.0 26.3 jit_solution(8268344528222584054)
XLA Ops:
  0.6 25.1 %decode.1 = (bf16[256,128]{1,0:T(8,128)(2,1)S(1)}, f32[1,8]{1,0:T(1,128)S(1)}) custom-call(s32[8]{0:T(128)} %anc_hbm.1, f32[8]{0:T(128)} %prior_hbm.1, f32[16,128]{1,0:T(8,128)} %vec_hbm.1, bf16[2,2,16,128]{3,2,1,0:T(8,128)(2,1)} %bitcast.9, bf16[256,128]{1,0:T(8,128)(2,1)} %bitcast.8, bf16[2,3584,128]{2,1,0:T(8,128)(2,1)} %bitcast.6, ...), custom_call_target="tpu_custom_call" | custom-call | tf_op jit(solution)/shard_map/decode/pallas_call | solution.py:379
  25.7 0.7 %write_out.1 = (bf16[256,128]{1,0:T(8,128)(2,1)}, f32[1,8]{1,0:T(1,128)}) custom-call(bf16[256,128]{1,0:T(8,128)(2,1)S(1)} %get-tuple-element.6.att_ref, f32[1,8]{1,0:T(1,128)S(1)} %get-tuple-element.7.lw_ref), custom_call_target="tpu_custom_call" | custom-call | tf_op jit(solution)/shard_map/write_out/pallas_call | solution.py:425

commit v3 on v2

--- a/solution.py
+++ b/solution.py
@@ -72,6 +72,16 @@
     mine = lax.axis_index("tensor")
     factor = math.log2(math.e) / math.sqrt(head)
 
+    def over(stop):
+        def run(body):
+            if stop > 16:
+                pl.loop(1, stop)(body)
+            else:
+                for k in range(1, stop):
+                    body(k)
+
+        return run
+
     def remote(src, dst, ssem, rsem, **where):
         return pltpu.make_async_remote_copy(
             src_ref=src, dst_ref=dst, send_sem=ssem, recv_sem=rsem,
@@ -80,13 +90,13 @@
 
     barrier = pltpu.get_barrier_semaphore()
 
-    @pl.loop(1, devices)
+    @over(devices)
     def _(k):
         pl.semaphore_signal(
             barrier, inc=1, device_id={"dp": lax.rem(me + k, devices)}, device_id_type=MESH
         )
 
-    @pl.loop(1, tensors)
+    @over(tensors)
     def _(k):
         pl.semaphore_signal(
             barrier, inc=1, device_id={"tensor": lax.rem(mine + k, tensors)}, device_id_type=MESH
@@ -137,7 +147,7 @@
     def s_copy(peer, slot):
         return remote(stat_send.at[peer], stat_recv.at[slot], s_ssem.at[peer], s_rsem.at[slot], dp=peer)
 
-    @pl.loop(1, devices)
+    @over(devices)
     def _(k):
         peer = lax.rem(me + k, devices)
         m_copy(peer, me).start()
@@ -158,7 +168,8 @@
     def _(i):
         at = pl.ds(pl.multiple_of(i * (chunk * kv_count), chunk * kv_count), chunk * kv_count)
         for c, part in enumerate(split(prompt_buf[0, at, :], chunk)):
-            keys[c, pl.ds(pl.multiple_of(i * chunk, chunk), chunk), :] = part.astype(jnp.bfloat16)
+            place = pl.ds(pl.multiple_of(i * chunk, chunk), chunk)
+            keys[place, c * head : (c + 1) * head] = part.astype(jnp.bfloat16)
 
     copy_v.wait()
 
@@ -174,7 +185,7 @@
     def _(i):
         at = pl.ds(pl.multiple_of(i * chunk, chunk), chunk)
         for c, part in enumerate(split(gen_buf[i, 0], chunk)):
-            gkeys[c, at, :] = part.astype(jnp.bfloat16)
+            gkeys[at, c * head : (c + 1) * head] = part.astype(jnp.bfloat16)
         for c, part in enumerate(split(gen_buf[i, 1], chunk)):
             gvals[c, :, at] = part.T.astype(jnp.bfloat16)
 
@@ -185,20 +196,34 @@
     def partial(slot, res, stat):
         ancestor = meta_all[slot, 0:1, :]
         held = (ancestor - (me * local).astype(jnp.float32)).astype(jnp.int32)
+        each = [rows_of(slot, c) for c in range(kv_count)]
+        blank = jnp.zeros((rows, head), jnp.bfloat16)
+        q = jnp.concatenate(
+            [
+                jnp.concatenate([each[c] if c == b else blank for b in range(kv_count)], axis=1)
+                for c in range(kv_count)
+            ],
+            axis=0,
+        )
+        held = jnp.concatenate([held] * kv_count, axis=1)
+        score = nt(keys[...], q)
+        tops = jnp.max(score, axis=0, keepdims=True)
+        weight = jnp.exp2((score - tops) * factor)
+        totals = jnp.sum(weight, axis=0, keepdims=True)
+        weight = weight.astype(jnp.bfloat16)
+        gscore = nt(gkeys[...], q).reshape(local, cached, kv_count * rows)
+        which = lax.broadcasted_iota(jnp.int32, (local, 1, kv_count * rows), 0)
+        gscore = jnp.where(which == held[None], gscore, MASKED)
+        gscore = gscore.reshape(local * cached, kv_count * rows)
+        gtops = jnp.max(gscore, axis=0, keepdims=True)
+        gweight = jnp.exp2((gscore - gtops) * factor)
+        gtotals = jnp.sum(gweight, axis=0, keepdims=True)
+        gweight = gweight.astype(jnp.bfloat16)
         for c in range(kv_count):
-            q = rows_of(slot, c)
-            score = nt(keys[c], q)
-            top = jnp.max(score, axis=0, keepdims=True)
-            weight = jnp.exp2((score - top) * factor)
-            total = jnp.sum(weight, axis=0, keepdims=True)
-            value = jnp.dot(vals[c], weight.astype(jnp.bfloat16), preferred_element_type=jnp.float32)
-            gscore = nt(gkeys[c], q).reshape(local, cached, rows)
-            which = lax.broadcasted_iota(jnp.int32, (local, 1, rows), 0)
-            gscore = jnp.where(which == held[None], gscore, MASKED).reshape(local * cached, rows)
-            gtop = jnp.max(gscore, axis=0, keepdims=True)
-            gweight = jnp.exp2((gscore - gtop) * factor)
-            gtotal = jnp.sum(gweight, axis=0, keepdims=True)
-            gvalue = jnp.dot(gvals[c], gweight.astype(jnp.bfloat16), preferred_element_type=jnp.float32)
+            span = slice(c * rows, (c + 1) * rows)
+            top, total, gtop, gtotal = tops[:, span], totals[:, span], gtops[:, span], gtotals[:, span]
+            value = jnp.dot(vals[c], weight[:, span], preferred_element_type=jnp.float32)
+            gvalue = jnp.dot(gvals[c], gweight[:, span], preferred_element_type=jnp.float32)
             both = jnp.maximum(top, gtop)
             one = jnp.exp2((top - both) * factor)
             two = jnp.exp2((gtop - both) * factor)
@@ -264,7 +289,7 @@
     before = lax.fori_loop(0, devices, add_before, jnp.zeros((local, head), jnp.float32))
     before = before * (mine == 0).astype(jnp.float32)
 
-    @pl.loop(1, devices)
+    @over(devices)
     def _(k):
         peer = lax.rem(me + devices - k, devices)
         s_copy(peer, peer).wait_recv()
@@ -313,11 +338,11 @@
         slot = place if slot is None else peer
         return remote(twist_own, twist_all.at[slot], t_ssem.at[peer], t_rsem.at[slot], **where)
 
-    @pl.loop(1, everyone)
+    @over(everyone)
     def _(k):
         t_copy(k, None).start()
 
-    @pl.loop(1, everyone)
+    @over(everyone)
     def _(k):
         t_copy(k, k).wait_recv()
 
@@ -339,7 +364,7 @@
     logs = of_device(me) - (largest + jnp.log(mass))
     lw_ref[...] = logs[:, :local]
 
-    @pl.loop(1, devices)
+    @over(devices)
     def _(k):
         peer = lax.rem(me + k, devices)
         m_copy(peer, me).wait_send()
@@ -347,7 +372,7 @@
         s_copy(peer, me).wait_send()
         r_copy(peer, me).wait_send()
 
-    @pl.loop(1, everyone)
+    @over(everyone)
     def _(k):
         t_copy(k, None).wait_send()
 
@@ -393,9 +418,9 @@
             pltpu.VMEM((2, positions * kv_count, head), bf16),
             pltpu.VMEM((local, 2, cached * kv_count, head), bf16),
             pltpu.VMEM((cached * kv_count, head), f32),
-            pltpu.VMEM((kv_count, positions, head), bf16),
+            pltpu.VMEM((positions, kv_count * head), bf16),
             pltpu.VMEM((kv_count, head, positions), bf16),
-            pltpu.VMEM((kv_count, local * cached, head), bf16),
+            pltpu.VMEM((local * cached, kv_count * head), bf16),
             pltpu.VMEM((kv_count, head, local * cached), bf16),
             pltpu.VMEM((devices, steps * local * heads, head), bf16),
             pltpu.VMEM((8, rows), f32),

time: 26.5 us -> 25.8 us (0.974)
  Pallas kernels: 25.7 us -> 25 us
    pallas_call x1, Pallas kernels: 25.1 us -> 24.4 us  [per_device(): pl.pallas_call(functools.partial(kernel, sizes), name='decode', out_shape...]
where the time goes in v3:
time: 25.8 us; the launch traced here: 25.6 us
  Pallas kernels  25 us (97%)
  between operations  0.64 us (2%)
    pallas_call x1, Pallas kernels, per_device(): pl.pallas_call(functools.partial(kernel, sizes), name='decode', out_shape...  24.4 us
    pallas_call x1, Pallas kernels, per_device(): pl.pallas_call(write_out, name='write_out', out_shape=(jax.ShapeDtypeStru...  0.65 us

profile of v3, /device:TPU:0, one launch (start us, length us, event | category | flops | bytes accessed | tf_op | source)
XLA Modules:
  0.0 25.6 jit_solution(9777146690691695172)
XLA Ops:
  0.6 24.4 %decode.1 = (bf16[256,128]{1,0:T(8,128)(2,1)S(1)}, f32[1,8]{1,0:T(1,128)S(1)}) custom-call(s32[8]{0:T(128)} %anc_hbm.1, f32[8]{0:T(128)} %prior_hbm.1, f32[16,128]{1,0:T(8,128)} %vec_hbm.1, bf16[2,2,16,128]{3,2,1,0:T(8,128)(2,1)} %bitcast.9, bf16[256,128]{1,0:T(8,128)(2,1)} %bitcast.8, bf16[2,3584,128]{2,1,0:T(8,128)(2,1)} %bitcast.6, ...), custom_call_target="tpu_custom_call" | custom-call | tf_op jit(solution)/shard_map/decode/pallas_call | solution.py:404
  25.0 0.7 %write_out.1 = (bf16[256,128]{1,0:T(8,128)(2,1)}, f32[1,8]{1,0:T(1,128)}) custom-call(bf16[256,128]{1,0:T(8,128)(2,1)S(1)} %get-tuple-element.6.att_ref, f32[1,8]{1,0:T(1,128)S(1)} %get-tuple-element.7.lw_ref), custom_call_target="tpu_custom_call" | custom-call | tf_op jit(solution)/shard_map/write_out/pallas_call | solution.py:450
